TPU v7x, 1024 devices: a whole 4x8x16 slice. The times are simulated.
1024 devices in a mesh: ia: 64 (over x, z_hi, y), ja: 16 (over z_lo, core).
Axes of the slice: x: 4, y: 8, z: 16 (z_hi: 2, z_lo: 8; z = z_hi * 8 + z_lo), core: 2. Of those that a mesh axis runs over, the one named last changes fastest.
Arguments:
- b_first: bfloat16 [64, 512, 1024], P('ia', None, 'ja'), may hold values from -0.63671875 to 0.63671875
- b_second: bfloat16 [32, 512, 1024], P('ja', None, 'ia'), may hold values from -0.63671875 to 0.63671875
- eps_first: float32 [64], P('ia'), may hold values from -2 to -0.3
- eps_second: float32 [32], P('ja'), may hold values from -2 to -0.3
- eps_virtual: float32 [512], replicated, may hold values from 0.1 to 3
- c_virtual: float32 [576, 512], replicated, may hold values from -0.25 to 0.25
- c_occupied: float32 [64, 576], replicated, may hold values from -0.75 to 0.75
Outputs:
- gamma_ao: float32 [576, 589824], P('ia', 'ja')
- density: float32 [512, 512], P('ia', 'ja')
All inputs are finite; a program needn't handle non-finite values.
Results may differ from a plain program's by a relative error of at most 0.0008.
Values may be sent and summed in bfloat16 or wider, within the bound.
A program may use at most 32 MiB of HBM per device.

v0:
```python
import jax
import jax.numpy as jnp
from jax import lax
from jax.sharding import Mesh
from jax.sharding import PartitionSpec as P

IA = ("ia_0", "ia_1", "ia_2")


def sent_to_all(array, axis):
    peers = lax.axis_size(axis)
    return lax.all_to_all(
        jnp.broadcast_to(array[None], (peers, *array.shape)), axis, 0, 0, tiled=True
    )


def laid_out(parts, dim):
    parts = jnp.moveaxis(parts, 0, dim)
    shape = parts.shape
    return parts.reshape(*shape[:dim], shape[dim] * shape[dim + 1], *shape[dim + 2 :])


def collect(array, axis, dim):
    parts = sent_to_all(array, axis)
    return laid_out(parts, dim)


def stacked_from(array, axes, turns):
    parts = array[None]
    for k in turns:
        parts = lax.all_gather(parts, axes[k], axis=0, tiled=True)
    carried = [lax.axis_size(axes[k]) for k in reversed(turns)]
    parts = parts.reshape(*carried, *array.shape)
    turned = sorted(range(len(turns)), key=lambda place: turns[len(turns) - 1 - place])
    return parts.transpose(*turned, *range(len(turns), parts.ndim)).reshape(-1, *array.shape)


def whole_of(array, axes, turns, dim):
    return laid_out(stacked_from(array, axes, turns), dim)


def split_up(array, dim, peers):
    shape = array.shape
    parts = array.reshape(*shape[:dim], peers, shape[dim] // peers, *shape[dim + 1 :])
    return jnp.moveaxis(parts, dim, 0)


def one_scatter(arrays, axis, dims):
    peers = lax.axis_size(axis)
    parts = [split_up(a, dim, peers) for a, dim in zip(arrays, dims)]
    lines = jnp.concatenate([b.reshape(peers, -1) for b in parts], axis=1)
    rows = max(16, -(-lines.shape[1] // 1024) * 8)
    lines = jnp.pad(lines, ((0, 0), (0, rows * 128 - lines.shape[1]))).reshape(-1, 128)
    line, at, outs = (lax.psum_scatter(lines, axis, tiled=True).reshape(-1), 0, [])
    for b in parts:
        part = b[0]
        outs.append(line[at : at + part.size].reshape(part.shape))
        at += part.size
    return tuple(outs)


def on_device(b_first, b_second, eps_first, eps_second, eps_virtual, c_virtual, c_occupied):
    n_first = b_first.shape[0] * lax.axis_size(IA)
    n_second = b_second.shape[0] * lax.axis_size("ja")
    first_full = collect(b_first, "ja", 2)
    second_full = whole_of(b_second, IA, (1, 0, 2), 2)
    integrals = jnp.einsum(
        "iap,jbp->ijab", first_full, second_full, preferred_element_type=jnp.float32
    )
    denominator = (
        eps_virtual[None, None, :, None]
        + eps_virtual[None, None, None, :]
        - eps_first[:, None, None, None]
        - eps_second[None, :, None, None]
    )
    amplitude = integrals / -denominator
    tilde = (2.0 * amplitude - jnp.swapaxes(amplitude, 2, 3)).astype(jnp.bfloat16)
    amp_round = amplitude.astype(jnp.bfloat16)
    gamma_part = jnp.einsum("ijab,jbp->iap", tilde, second_full, preferred_element_type=jnp.float32)
    density_part = jnp.einsum("ijac,ijbc->ab", tilde, amp_round, preferred_element_type=jnp.float32)
    gamma_local, density_local = one_scatter((gamma_part, density_part), "ja", (2, 1))
    virtual_back = jnp.einsum(
        "na,iap->inp", c_virtual, gamma_local, precision=lax.Precision.HIGHEST
    )
    stacked = density_local.reshape(1, density_local.shape[0], density_local.shape[1])
    gathered, pieces_all = (
        lax.all_to_all(virtual_back, IA, split_axis=1, concat_axis=0, tiled=True),
        lax.all_to_all(stacked, IA, split_axis=1, concat_axis=0, tiled=True),
    )
    density = jnp.sum(pieces_all, axis=0)
    gamma_ao = jnp.einsum("im,inp->npm", c_occupied, gathered, precision=lax.Precision.HIGHEST)
    gamma_ao = gamma_ao.reshape(gamma_ao.shape[0], gamma_ao.shape[1] * gamma_ao.shape[2])
    return (gamma_ao, density / (n_first * n_second))


def solution(mesh):
    torus = Mesh(mesh.devices.reshape(4, 2, 8, mesh.shape["ja"]), ("ia_0", "ia_1", "ia_2", "ja"))
    return jax.shard_map(
        on_device,
        mesh=torus,
        in_specs=(P(IA, None, "ja"), P("ja", None, IA), P(IA), P("ja"), P(), P(), P()),
        out_specs=(P(IA, "ja"), P(IA, "ja")),
        check_vma=False,
    )
```

profile of v0, /device:TPU:1, one launch (start us, length us, event | category | flops | bytes accessed | tf_op | source)
XLA Modules:
  0.0 364.6 jit_solution(12423823087364790148)
XLA Ops:
  7.2 2.0 broadcast_in_dim.8
  9.2 17.6 %all-to-all-start = ((bf16[16,1,512,64]{2,3,1,0:T(8,128)(2,1)}), bf16[16,1,512,64]{2,3,1,0:T(8,128)(2,1)S(1)}, u32[]{:S(2)}, u32[]{:S(2)}) async-start(bf16[16,1,512,64]{2,3,1,0:T(8,128)(2,1)} %broadcast_in_dim.8), calls=%async_computation | async-start | bytes 2097152 | tf_op jit(solution)/shard_map/all_to_all | solution.py:12
  26.8 31.7 %all-gather = bf16[4,512,16]{1,2,0:T(8,128)(2,1)S(1)} all-gather(bf16[2,512,16]{1,2,0:T(8,128)(2,1)S(1)} %copy-done.4), channel_id=2, replica_groups=mesh['ia_0'=4,'ia_1'=2,'ia_2'=8,'ja'=16] {'ia_1'}, dimensions={0}, use_global_device_ids=true | all-gather | bytes 98304 | tf_op jit(solution)/shard_map/all_gather | solution.py:31
  58.6 11.1 %all_gather.10 = bf16[8,2,512,16]{2,3,1,0:T(8,128)(2,1)} all-gather(bf16[2,2,512,16]{2,3,1,0:T(8,128)(2,1)S(1)} %bitcast.101), channel_id=1, replica_groups=mesh['ia_0'=4,'ia_1'=2,'ia_2'=8,'ja'=16] {'ia_0'}, dimensions={0}, use_global_device_ids=true | all-gather | bytes 327680 | tf_op jit(solution)/shard_map/all_gather | solution.py:31
  70.4 1.2 add_subtract_fusion
  71.6 65.0 %all-gather.3.cloned.1.call-done = bf16[64,2,512,16]{2,3,1,0:T(8,128)(2,1)} async-done(((bf16[8,2,512,16]{2,3,1,0:T(8,128)(2,1)}), bf16[64,2,512,16]{2,3,1,0:T(8,128)(2,1)}) %all-gather.3.cloned.1.call-update) | async-done | bytes 2097168 | tf_op jit(solution)/shard_map/all_gather | solution.py:31
  136.6 1.8 copy.52
  138.4 1.5 copy.53
  139.9 1.0 copy-done.2
  140.9 4.5 %fusion.6 = (bf16[1,2,512,512]{3,2,1,0:T(8,128)(2,1)}, f32[1,2,512,512]{3,2,1,0:T(8,128)S(1)}) fusion(f32[2]{0:T(128)S(1)} %copy-done.6, f32[512,512]{1,0:T(8,128)} %add_subtract_fusion, bf16[2,512,1024]{1,2,0:T(8,128)(2,1)} %bitcast.94, bf16[512,1024,1]{0,1,2:T(8,128)(2,1)} %bitcast.100), kind=kOutput, calls=%fused_computation.14 | convolution fusion | flops 1075838976 | bytes 7340040 | tf_op jit(solution)/shard_map/iap,jbp->ijab/dot_general | solution.py:67
  145.4 1.9 copy.57
  147.2 2.2 fusion
  149.5 1.0 copy-done.1
  151.2 2.6 copy.63
  153.8 4.3 %reshape.125 = f32[16,16384]{1,0:T(8,128)} reshape(f32[16,512,32]{2,1,0:T(8,128)} %copy.63) | data formatting | bytes 2097152 | tf_op jit(solution)/shard_map/reshape | solution.py:51
  158.2 3.2 convolution_bitcast_fusion
  161.3 2.7 copy.60
  164.0 2.9 reshape.123
  167.0 3.1 pad_maximum_fusion
  170.0 3.3 reshape.126
  173.4 112.7 %reduce-scatter.2.cloned.1.call-done = f32[384,128]{1,0:T(8,128)} async-done(((f32[6144,128]{1,0:T(8,128)}), f32[384,128]{1,0:T(8,128)}) %reduce-scatter.2.cloned.1.call-update) | async-done | bytes 196624 | tf_op jit(solution)/shard_map/reduce_scatter | solution.py:54
  287.6 1.3 reduce.9
  289.7 18.7 %all-to-all-start.2 = ((f32[64,1,256]{2,1,0:T(1,128)}), f32[64,1,256]{2,1,0:T(1,128)S(1)}, u32[]{:S(2)}, u32[]{:S(2)}) async-start(f32[64,1,256]{2,1,0:T(1,128)} %reshape.147), calls=%async_computation.3 | async-start | bytes 131072 | tf_op jit(solution)/shard_map/all_to_all | solution.py:88
  309.4 1.4 convolution_bitcast_fusion.2
  311.0 1.4 reduce.7
  313.2 12.9 %all-to-all-done.2 = f32[64,1,256]{2,1,0:T(1,128)S(1)} async-done(((f32[64,1,256]{2,1,0:T(1,128)}), f32[64,1,256]{2,1,0:T(1,128)S(1)}, u32[]{:S(2)}, u32[]{:S(2)}) %all-to-all-start.2) | async-done | bytes 65568 | tf_op jit(solution)/shard_map/all_to_all | solution.py:88
  326.2 6.3 %all-to-all-start.1 = ((f32[64,1,576]{2,1,0:T(1,128)}), f32[64,1,576]{2,1,0:T(1,128)S(1)}, u32[]{:S(2)}, u32[]{:S(2)}) async-start(f32[64,1,576]{2,1,0:T(1,128)} %reshape.145), calls=%async_computation.2 | async-start | bytes 327680 | tf_op jit(solution)/shard_map/all_to_all | solution.py:87
  334.4 16.5 %all-to-all-done.1 = f32[64,1,576]{2,1,0:T(1,128)S(1)} async-done(((f32[64,1,576]{2,1,0:T(1,128)}), f32[64,1,576]{2,1,0:T(1,128)S(1)}, u32[]{:S(2)}, u32[]{:S(2)}) %all-to-all-start.1) | async-done | bytes 147488 | tf_op jit(solution)/shard_map/all_to_all | solution.py:87
  350.9 1.0 reduce.8
  352.8 1.4 bitcast_reduce_fusion
  354.2 1.4 fusion.3
  355.6 2.2 reshape.128
  (35 shorter events, 7.9 us)
Async XLA Ops:
  7.2 302.2 %copy-start = (f32[576,512]{1,0:T(8,128)S(1)}, f32[576,512]{1,0:T(8,128)}, u32[]{:S(2)}) copy-start(f32[576,512]{1,0:T(8,128)} %param.12) | copy-start | bytes 3538948
  7.2 19.6 %copy-start.4 = (bf16[2,512,16]{1,2,0:T(8,128)(2,1)S(1)}, bf16[2,512,16]{1,2,0:T(8,128)(2,1)}, u32[]{:S(2)}) copy-start(bf16[2,512,16]{1,2,0:T(8,128)(2,1)} %param.8) | copy-start | bytes 98308
  7.2 63.2 %copy-start.5 = (f32[512]{0:T(512)S(1)}, f32[512]{0:T(512)}, u32[]{:S(2)}) copy-start(f32[512]{0:T(512)} %param.11) | copy-start | bytes 6148
  9.2 130.7 %all-to-all-start = ((bf16[16,1,512,64]{2,3,1,0:T(8,128)(2,1)}), bf16[16,1,512,64]{2,3,1,0:T(8,128)(2,1)S(1)}, u32[]{:S(2)}, u32[]{:S(2)}) async-start(bf16[16,1,512,64]{2,3,1,0:T(8,128)(2,1)} %broadcast_in_dim.8), calls=%async_computation | async-start | bytes 2097152 | tf_op jit(solution)/shard_map/all_to_all | solution.py:12
  26.8 109.8 %all-gather.3.cloned.1.call-start = ((), (), s32[]{:S(2)}) async-start(), calls=%async_computation.4 | async-start | bytes 2359296 | tf_op jit(solution)/shard_map/all_gather | solution.py:31
  69.7 216.4 %reduce-scatter.2.cloned.1.call-start = ((), (), s32[]{:S(2)}) async-start(), calls=%async_computation.5 | async-start | bytes 3342336 | tf_op jit(solution)/shard_map/reduce_scatter | solution.py:54
  138.4 2.5 copy-start.6
  139.9 1.0 copy-start.2
  147.2 3.2 copy-start.7
  149.5 1.0 copy-start.1
  289.7 36.5 %all-to-all-start.2 = ((f32[64,1,256]{2,1,0:T(1,128)}), f32[64,1,256]{2,1,0:T(1,128)S(1)}, u32[]{:S(2)}, u32[]{:S(2)}) async-start(f32[64,1,256]{2,1,0:T(1,128)} %reshape.147), calls=%async_computation.3 | async-start | bytes 131072 | tf_op jit(solution)/shard_map/all_to_all | solution.py:88
  311.0 43.2 %copy-start.3 = (f32[64,576]{1,0:T(8,128)S(1)}, f32[64,576]{1,0:T(8,128)}, u32[]{:S(2)}) copy-start(f32[64,576]{1,0:T(8,128)} %param.13) | copy-start | bytes 442372
  326.2 24.8 %all-to-all-start.1 = ((f32[64,1,576]{2,1,0:T(1,128)}), f32[64,1,576]{2,1,0:T(1,128)S(1)}, u32[]{:S(2)}, u32[]{:S(2)}) async-start(f32[64,1,576]{2,1,0:T(1,128)} %reshape.145), calls=%async_computation.2 | async-start | bytes 327680 | tf_op jit(solution)/shard_map/all_to_all | solution.py:87
Sparse Core Ops, SparseCore 0:
  69.8 66.6 all-gather.2
  173.5 112.4 reduce-scatter.1
where the time goes:
time: 368 us; the launch traced here: 365 us
  waiting for transfers between devices  207 us (56%)
  blocking collectives  42.9 us (12%)
  starting transfers between devices  42.6 us (12%)
  local copies, waits for them, and re-layouts  34.3 us (9%)
  between operations  14.9 us (4%)
  other arithmetic  11.6 us (3%)
  matrix products  11.1 us (3%)
    reduce_scatter x1, waiting for transfers between devices, one_scatter(): lax.psum_scatter(lines, axis, tiled=True).reshape(-1)  113 us
    all_gather x1, waiting for transfers between devices, stacked_from(): parts = lax.all_gather(parts, axes[k], axis=0, tiled=True)  65 us
    all_gather x2, blocking collectives, stacked_from(): parts = lax.all_gather(parts, axes[k], axis=0, tiled=True)  42.9 us
    all_to_all x1, starting transfers between devices, on_device(): lax.all_to_all(stacked, IA, split_axis=1, concat_axis=0, tiled=True)  18.7 us
    all_to_all x1, starting transfers between devices, sent_to_all(): lax.all_to_all(jnp.broadcast_to(array[None], (peers, *array.shape)), axis...  17.6 us
    all_to_all x1, waiting for transfers between devices, on_device(): lax.all_to_all(virtual_back, IA, split_axis=1, concat_axis=0, tiled=True)  16.5 us
    all_to_all x1, waiting for transfers between devices, on_device(): lax.all_to_all(stacked, IA, split_axis=1, concat_axis=0, tiled=True)  12.9 us
  transfers between devices with their start and end apart: 5, of which 4 were waited for; matrix products, arithmetic and copies ran while one was open for 3% of the time, Pallas kernels for 0%

commit v1 on v0

v1 whole, which is shorter than its diff:
```python
import jax
import jax.numpy as jnp
from jax import lax
from jax.experimental import pallas as pl
from jax.experimental.pallas import tpu as pltpu
from jax.sharding import PartitionSpec as P

F32, BF16 = jnp.float32, jnp.bfloat16
MESH = pl.DeviceIdType.MESH
NX, NY, NH, NL, NZ = 4, 8, 2, 8, 16
PLANE = NX * NY
CR = 72
BR = 9


def dot(a, b, ca, cb):
    return lax.dot_general(a, b, (((ca,), (cb,)), ((), ())), preferred_element_type=F32)


def split(v):
    hi = v.astype(BF16)
    return hi, (v - hi.astype(F32)).astype(BF16)


def place():
    ia, ja = lax.axis_index("ia"), lax.axis_index("ja")
    return ia // 16, (ia // 8) % 2, ia % 8, ja // 2, ja % 2


def dev(x, y, z, c):
    return ((x * 2 + z // 8) * 8 + y, (z % 8) * 2 + c)


def remote(src, dst, ss, rs, to):
    return pltpu.make_async_remote_copy(
        src_ref=src, dst_ref=dst, send_sem=ss, recv_sem=rs, device_id=to, device_id_type=MESH
    )


def main_kernel(
    bf, bs, e1, e2, ev, cv,
    R, dens_out,
    F, S, E, Chi, Clo, T, AR, Ghi, Glo, D, DP, DY, DX, DZ, DR, DO, QR, QL, SB,
    f0_s, f0_r, fr_s, fr_r, fl_s, fl_r,
    w_s, w_r, sx_s, sx_r, yr_s, yr_r, yl_s, yl_r, pc_s, pc_r, e_s, e_r,
    qr_s, qr_r, ql_s, ql_r, dp_s, dp_r, dy_s, dy_r, dx_s, dx_r, dz_s, dz_r, do_s, do_r,
    a_s, a_r, r_s, r_r, loc,
):
    x, h, y, l, c = place()
    z = h * 8 + l
    k = 1 - c
    ip = x * 8 + y
    ja = l * 2 + c
    home = c == h
    mate = dev(x, y, z, k)
    far = lax.rem(z + 8, NZ)

    E[0, 0] = jnp.full((8, 128), e1[0], F32)
    E[0, 1] = jnp.full((8, 128), e2[0], F32)
    E[0, 2] = jnp.full((8, 128), e2[1], F32)
    barrier = pltpu.get_barrier_semaphore()

    def hail(to):
        pl.semaphore_signal(barrier, inc=1, device_id=to, device_id_type=MESH)

    hail(mate)
    hail(dev(x, y, far, k))

    @pl.loop(1, NZ)
    def _(d):
        hail(dev(x, y, lax.rem(z + d, NZ), c))

    @pl.loop(1, PLANE)
    def _(d):
        q = lax.rem(ip + d, PLANE)
        hail(dev(q // 8, q % 8, z, c))

    pl.semaphore_wait(barrier, 2 + NZ - 1 + PLANE - 1)

    e_far = remote(E.at[0], E.at[1], e_s.at[0], e_r.at[0], dev(x, y, far, c))
    e_mate = remote(E.at[0], E.at[2], e_s.at[1], e_r.at[1], mate)
    s_own = [S.at[j, x, h, y] for j in range(2)]

    @pl.when(home)
    def _():
        remote(bs.at[k], S.at[k, x, h, y], w_s.at[0], w_r.at[0], mate).start()
        pltpu.make_async_copy(bs.at[c], S.at[c, x, h, y], loc.at[0]).start()
        pltpu.make_async_copy(bf, F.at[ja], loc.at[1]).start()

    @pl.when(jnp.logical_not(home))
    def _():
        remote(bf, F.at[ja], f0_s, f0_r, mate).start()
        remote(bs.at[c], S.at[c, x, h, y], w_s.at[0], w_r.at[1], dev(x, y, far, c)).start()
        remote(bs.at[k], S.at[k, x, h, y], w_s.at[1], w_r.at[1], dev(x, y, far, k)).start()

    e_far.start()
    e_mate.start()

    def split_c(g):
        hi, lo = split(cv[g])
        Chi[g] = hi
        Clo[g] = lo

    pl.loop(0, 8)(split_c)

    def x_sends(hp, slot):
        for d in range(1, NX):
            to = lax.rem(x + d, NX)
            piece = S.at[c, x, hp, y]
            remote(piece, piece, sx_s.at[slot, d - 1], sx_r.at[slot, d - 1], dev(to, y, z, c)).start()

    def x_waits(hp, slot):
        for d in range(1, NX):
            frm = lax.rem(x + NX - d, NX)
            piece = S.at[c, frm, hp, y]
            remote(piece, piece, sx_s.at[slot, d - 1], sx_r.at[slot, d - 1], mate).wait_recv()
        for d in range(1, NX):
            piece = S.at[c, x, hp, y]
            remote(piece, piece, sx_s.at[slot, d - 1], sx_r.at[slot, d - 1], mate).wait_send()

    yr, yl = lax.rem(y + 1, NY), lax.rem(y + NY - 1, NY)

    def y_block(hp, yo):
        return S.at[c, :, hp, yo]

    def y_copy(hp, slot, s, right):
        yo = lax.rem(y + NY - s, NY) if right else lax.rem(y + s, NY)
        b = y_block(hp, yo)
        ss, rs = (yr_s, yr_r) if right else (yl_s, yl_r)
        return remote(b, b, ss.at[slot, s], rs.at[slot, s], dev(x, yr if right else yl, z, c))

    def y_got(hp, slot, s, right):
        yo = lax.rem(y + NY - s, NY) if right else lax.rem(y + s, NY)
        b = y_block(hp, yo)
        ss, rs = (yr_s, yr_r) if right else (yl_s, yl_r)
        remote(b, b, ss.at[slot, s - 1], rs.at[slot, s - 1], mate).wait_recv()

    def share(hp, slot, n, yo):
        b = y_block(hp, yo)
        remote(b, b, pc_s.at[slot, n], pc_r.at[slot, n], mate).start()

    def y_step(hp, slot, s):
        if s == 0:
            y_copy(hp, slot, 0, True).start()
            y_copy(hp, slot, 0, False).start()
            share(hp, slot, 0, y)
            return
        y_got(hp, slot, s, True)
        if s < 4:
            y_copy(hp, slot, s, True).start()
        share(hp, slot, s, lax.rem(y + NY - s, NY))
        if s < 4:
            y_got(hp, slot, s, False)
            if s < 3:
                y_copy(hp, slot, s, False).start()
            share(hp, slot, 4 + s, lax.rem(y + s, NY))

    zr, zl = lax.rem(z + 1, NZ), lax.rem(z + NZ - 1, NZ)

    def f_step(s):
        for right in (True, False):
            last = 8 if right else 7
            if s > last:
                continue
            o = lax.rem(z + NZ - s, NZ) if right else lax.rem(z + s, NZ)
            ss, rs = (fr_s, fr_r) if right else (fl_s, fl_r)
            to = dev(x, y, zr if right else zl, c)

            @pl.when(o // 8 == c)
            def _():
                for q in range(2):
                    b = F.at[lax.rem(o, NL) * 2 + q]
                    if s > 0:
                        remote(b, b, ss.at[s - 1, q], rs.at[s - 1, q], to).wait_recv()
                    if s < last:
                        remote(b, b, ss.at[s, q], rs.at[s, q], to).start()

    @pl.when(home)
    def _():
        pltpu.make_async_copy(bs.at[c], S.at[c, x, h, y], loc.at[0]).wait()
        pltpu.make_async_copy(bf, F.at[ja], loc.at[1]).wait()
        remote(bf, F.at[l * 2 + k], f0_s, f0_r, mate).wait_recv()

    @pl.when(jnp.logical_not(home))
    def _():
        remote(bs.at[c], S.at[c, x, h, y], w_s.at[0], w_r.at[0], mate).wait_recv()

    other = 1 - h
    x_sends(h, 0)
    f_step(0)
    x_waits(h, 0)
    y_step(h, 0, 0)
    f_step(1)
    y_step(h, 0, 1)
    f_step(2)
    y_step(h, 0, 2)
    remote(bs.at[c], S.at[c, x, other, y], w_s.at[0], w_r.at[1], mate).wait_recv()
    x_sends(other, 1)
    f_step(3)
    y_step(h, 0, 3)
    x_waits(other, 1)
    y_step(other, 1, 0)
    f_step(4)
    y_step(h, 0, 4)
    y_step(other, 1, 1)
    f_step(5)
    y_step(other, 1, 2)
    f_step(6)
    y_step(other, 1, 3)
    f_step(7)
    y_step(other, 1, 4)
    f_step(8)

    e_far.wait()
    e_mate.wait()
    for slot, hp in ((0, h), (1, other)):
        for n in range(NY):
            b = S.at[k, :, hp, n]
            remote(b, b, pc_s.at[slot, n], pc_r.at[slot, n], mate).wait_recv()

    ei = jnp.where(home, E[0, 0, 0:1, 0:1], E[1, 0, 0:1, 0:1])
    row = ev[...]
    for j in range(2):
        ej = jnp.where(home, E[0, 1 + j, 0:1, 0:1], E[2, 1 + j, 0:1, 0:1])

        @pl.loop(0, 4)
        def _(t):
            cols = pl.ds(pl.multiple_of(t * 128, 128), 128)
            full_s = S[j].reshape(1024, 512)
            full_f = F[...].reshape(1024, 512)
            tile_f = F[:, :, cols].reshape(1024, 128)
            tile_s = S[j, :, :, :, :, cols].reshape(1024, 128)
            i_ab = dot(tile_f, full_s, 0, 0)
            i_ba = dot(tile_s, full_f, 0, 0)
            col = jnp.transpose(jnp.broadcast_to(ev[:, cols], (128, 128)))[:, 0:1]
            r = 1.0 / (ei + ej - (col + row))
            a = i_ab * r
            at = i_ba * r
            rows = pl.ds(pl.multiple_of(t * 128, 128), 128)
            T[j, rows, :] = (2.0 * a - at).astype(BF16)
            AR[j, rows, :] = at.astype(BF16)

    @pl.loop(0, 8)
    def _(g):
        gx, gh = g // 2, g % 2
        acc = dot(T[0], S[0, gx, gh].reshape(128, 512), 1, 1)
        acc += dot(T[1], S[1, gx, gh].reshape(128, 512), 1, 1)
        hi, lo = split(acc)
        Ghi[g] = hi
        Glo[g] = lo

    def own(d, q):
        hd, ld = d // 8, d % 8
        ghi, glo = Ghi[ld], Glo[ld]
        out = []
        for xi in (2 * q, 2 * q + 1):
            chi, clo = Chi[xi * 2 + hd], Clo[xi * 2 + hd]
            out.append(dot(chi, ghi, 1, 0) + dot(clo, ghi, 1, 0) + dot(chi, glo, 1, 0))
        return jnp.concatenate(out, axis=0)

    def q_copy(buf, s, q, right):
        ss, rs = (qr_s, qr_r) if right else (ql_s, ql_r)
        return remote(
            buf.at[s, q], buf.at[s + 1, q], ss.at[s, q], rs.at[s, q], dev(x, y, zr if right else zl, c)
        )

    for right, buf in ((True, QR), (False, QL)):
        d0 = lax.rem(z + (8 if right else 9), NZ)
        for q in range(2):
            buf[0, q] = own(d0, q)
            q_copy(buf, 0, q, right).start()

    def q_steps(lo, hi):
        @pl.loop(lo, hi)
        def _(s):
            dr = lax.rem(z + 8 + NZ - s, NZ)
            dl = lax.rem(z + 9 + s, NZ)
            for right, buf, d in ((True, QR, dr), (False, QL, dl)):
                for q in range(2):
                    mine = own(d, q)
                    q_copy(buf, s - 1, q, right).wait_recv()
                    buf[s, q] += mine
                    q_copy(buf, s, q, right).start()

    for t in range(4):
        acc = dot(T[0, t * 128 : t * 128 + 128, :], AR[0], 1, 0)
        acc += dot(T[1, t * 128 : t * 128 + 128, :], AR[1], 1, 0)
        D[t // 2, (t % 2) * 2 : (t % 2) * 2 + 2] = acc.reshape(2, 8, 8, 512)
    d_mate = remote(D.at[k], DP, dp_s, dp_r, mate)
    d_mate.start()

    q_steps(1, 2)

    d_mate.wait_recv()

    @pl.loop(0, NY)
    def _(yy):
        D[c, :, yy] += DP[:, yy]

    for d in range(1, NY):
        to = lax.rem(y + d, NY)
        remote(D.at[c, :, to], DY.at[d - 1], dy_s.at[d - 1], dy_r.at[d - 1], dev(x, to, z, c)).start()

    q_steps(2, 5)

    total = D[c, :, y]
    for d in range(1, NY):
        remote(D.at[c, :, 0], DY.at[d - 1], dy_s.at[d - 1], dy_r.at[d - 1], mate).wait_recv()
        total += DY[d - 1]
    for i in range(2):
        DX[0, i] = total[2 * i : 2 * i + 2]
    act = x // 2 == c
    for i in range(2):

        @pl.when(2 * c + i != x)
        def _():
            to = 2 * c + i
            slot = lax.rem(x + NX - to, NX)
            remote(DX.at[0, i], DX.at[slot, 0], dx_s.at[i], dx_r.at[slot], dev(to, y, z, c)).start()

    q_steps(5, 6)

    @pl.when(act)
    def _():
        tot = DX[0, x - 2 * c]
        for slot in range(1, NX):
            remote(DX.at[0, 0], DX.at[slot, 0], dx_s.at[0], dx_r.at[slot], mate).wait_recv()
            tot += DX[slot, 0]
        for t in range(4):
            DZ[:, t] = tot[:, :, t * 128 : t * 128 + 128]
        DR[0] = DZ[h, l // 2]

        for d in range(1, NZ):
            zt = lax.rem(z + d, NZ)
            remote(
                DZ.at[zt // 8, (zt % 8) // 2], DR.at[d], dz_s.at[d], dz_r.at[d], dev(x, y, zt, c)
            ).start()

    q_steps(6, 7)
    for q in range(2):
        mine = own(lax.rem(z + 1, NZ), q)
        q_copy(QR, 6, q, True).wait_recv()
        QR[7, q] += mine
        q_copy(QR, 7, q, True).start()
    for q in range(2):
        mine = own(z, q)
        q_copy(QL, 6, q, False).wait_recv()
        QL[7, q] += mine
    for q in range(2):
        q_copy(QR, 7, q, True).wait_recv()
        got = QR[8, q] + QL[7, q]
        for i in range(16):
            SB[q * 16 + i, 0:BR] = got[i * BR : i * BR + BR]
        for i in range(16):
            b = q * 16 + i

            @pl.when(b != ip)
            def _():
                remote(SB.at[b], R.at[c, ip], a_s.at[b], a_r.at[ip], dev(b // 8, b % 8, z, c)).start()

    R[c, ip] = SB[ip]

    @pl.when(act)
    def _():
        tile = DR[0]
        for d in range(1, NZ):
            remote(DR.at[0], DR.at[d], dz_s.at[d], dz_r.at[d], mate).wait_recv()
            tile += DR[d]
        DO[...] = tile
        remote(DO, DO, do_s, do_r, mate).start()

    @pl.loop(1, PLANE)
    def _(d):
        b = lax.rem(ip + d, PLANE)
        remote(SB.at[b], R.at[c, b], a_s.at[b], a_r.at[b], mate).wait_recv()

    half = remote(R.at[c], R.at[c], r_s, r_r, mate)
    half.start()

    @pl.when(jnp.logical_not(act))
    def _():
        remote(DO, DO, do_s, do_r, mate).wait_recv()

    dens_out[...] = DO[...]

    @pl.when(home)
    def _():
        remote(bs.at[k], S.at[k, x, h, y], w_s.at[0], w_r.at[0], mate).wait_send()

    @pl.when(jnp.logical_not(home))
    def _():
        remote(bf, F.at[ja], f0_s, f0_r, mate).wait_send()
        remote(bs.at[c], S.at[c, x, h, y], w_s.at[0], w_r.at[1], mate).wait_send()
        remote(bs.at[k], S.at[k, x, h, y], w_s.at[1], w_r.at[1], mate).wait_send()

    for right in (True, False):
        ss = fr_s if right else fl_s
        for s in range(8 if right else 7):
            o = lax.rem(z + NZ - s, NZ) if right else lax.rem(z + s, NZ)

            @pl.when(o // 8 == c)
            def _():
                for q in range(2):
                    b = F.at[lax.rem(o, NL) * 2 + q]
                    remote(b, b, ss.at[s, q], fr_r.at[s, q], mate).wait_send()

    for slot in range(2):
        for s in range(4):
            y_copy(h, slot, s, True).wait_send()
            if s < 3:
                y_copy(h, slot, s, False).wait_send()
        for n in range(NY):
            b = y_block(h, 0)
            remote(b, b, pc_s.at[slot, n], pc_r.at[slot, n], mate).wait_send()
    for s in range(8):
        for q in range(2):
            q_copy(QR, s, q, True).wait_send()
            if s < 7:
                q_copy(QL, s, q, False).wait_send()
    d_mate.wait_send()
    for d in range(1, NY):
        remote(D.at[c, :, 0], DY.at[d - 1], dy_s.at[d - 1], dy_r.at[d - 1], mate).wait_send()
    for i in range(2):

        @pl.when(2 * c + i != x)
        def _():
            remote(DX.at[0, i], DX.at[1, 0], dx_s.at[i], dx_r.at[1], mate).wait_send()

    @pl.when(act)
    def _():
        for d in range(1, NZ):
            remote(DR.at[0], DR.at[d], dz_s.at[d], dz_r.at[d], mate).wait_send()
        remote(DO, DO, do_s, do_r, mate).wait_send()

    @pl.loop(1, PLANE)
    def _(d):
        b = lax.rem(ip + d, PLANE)
        remote(SB.at[b], R.at[c, b], a_s.at[b], a_r.at[b], mate).wait_send()

    half.wait_send()
    remote(R.at[k], R.at[k], r_s, r_r, mate).wait_recv()


def last_kernel(r, co, dens, gamma, density, W, L):
    _, _, _, l, c = place()
    W[...] = jnp.zeros_like(W)
    for hi in range(2):
        for x in range(NX):
            rows = co[(x * 2 + hi) * 8 : (x * 2 + hi) * 8 + 8, :]
            at = hi * 32 + x * 8
            W[at : at + 8, 0:576] = rows
            W[64 + at : 64 + at + 8, 576:1152] = rows
    w_hi, w_lo = split(W[...])
    for n in range(BR):
        both = jnp.transpose(r[:, :, n, :].reshape(64, 128))
        L[0, n], L[1, n] = both[0:64], both[64:128]
    for n in range(BR):
        even = L[c, n, pl.ds(0, 32, stride=2), :]
        odd = L[c, n, pl.ds(1, 32, stride=2), :]
        l_hi, l_lo = split(jnp.concatenate([even, odd], axis=1))
        res = dot(l_hi, w_hi, 1, 0) + dot(l_lo, w_hi, 1, 0) + dot(l_hi, w_lo, 1, 0)
        for t in range(32):
            gamma[n : n + 1, t * 1152 : t * 1152 + 1152] = res[t : t + 1, :]
    at = (l % 2) * 64 + c * 32
    turned = pltpu.roll(dens[...], lax.rem(128 - at, 128), 1)
    density[...] = turned[:, 0:32] * (1.0 / 2048.0)


def on_device(b_first, b_second, eps_first, eps_second, eps_virtual, c_virtual, c_occupied):
    bf = jnp.swapaxes(b_first, 1, 2)[0]
    bs = jnp.swapaxes(b_second, 1, 2)
    dma = pltpu.SemaphoreType.DMA
    vm = pl.BlockSpec(memory_space=pltpu.VMEM)
    sm = pl.BlockSpec(memory_space=pltpu.SMEM)
    r, dens = pl.pallas_call(
        main_kernel,
        out_shape=(
            jax.ShapeDtypeStruct((2, PLANE, 16, 128), F32),
            jax.ShapeDtypeStruct((8, 128), F32),
        ),
        in_specs=[vm, vm, sm, sm, vm, vm],
        out_specs=(vm, vm),
        scratch_shapes=[
            pltpu.VMEM((16, 64, 512), BF16),
            pltpu.VMEM((2, NX, NH, NY, 16, 512), BF16),
            pltpu.VMEM((3, 3, 8, 128), F32),
            pltpu.VMEM((8, CR, 512), BF16),
            pltpu.VMEM((8, CR, 512), BF16),
            pltpu.VMEM((2, 512, 512), BF16),
            pltpu.VMEM((2, 512, 512), BF16),
            pltpu.VMEM((8, 512, 128), BF16),
            pltpu.VMEM((8, 512, 128), BF16),
            pltpu.VMEM((2, 4, 8, 8, 512), F32),
            pltpu.VMEM((4, 8, 8, 512), F32),
            pltpu.VMEM((7, 4, 8, 512), F32),
            pltpu.VMEM((4, 2, 2, 8, 512), F32),
            pltpu.VMEM((2, 4, 8, 128), F32),
            pltpu.VMEM((16, 8, 128), F32),
            pltpu.VMEM((8, 128), F32),
            pltpu.VMEM((9, 2, 144, 128), F32),
            pltpu.VMEM((8, 2, 144, 128), F32),
            pltpu.VMEM((PLANE, 16, 128), F32),
            dma, dma, dma((8, 2)), dma((8, 2)), dma((7, 2)), dma((7, 2)),
            dma((2,)), dma((2,)), dma((2, 3)), dma((2, 3)),
            dma((2, 4)), dma((2, 4)), dma((2, 3)), dma((2, 3)), dma((2, 8)), dma((2, 8)),
            dma((2,)), dma((2,)),
            dma((8, 2)), dma((8, 2)), dma((7, 2)), dma((7, 2)), dma, dma, dma((7,)), dma((7,)),
            dma((2,)), dma((4,)), dma((16,)), dma((16,)), dma, dma,
            dma((PLANE,)), dma((PLANE,)), dma, dma, dma((2,)),
        ],
        compiler_params=pltpu.CompilerParams(
            collective_id=0, has_side_effects=True, vmem_limit_bytes=48 << 20
        ),
        name="pairs",
    )(bf, bs, eps_first, eps_second, eps_virtual.reshape(1, 512), c_virtual.reshape(8, CR, 512))
    return pl.pallas_call(
        last_kernel,
        out_shape=(
            jax.ShapeDtypeStruct((BR, 36864), F32),
            jax.ShapeDtypeStruct((8, 32), F32),
        ),
        in_specs=[vm, vm, vm],
        out_specs=(vm, vm),
        scratch_shapes=[pltpu.VMEM((128, 1152), F32), pltpu.VMEM((2, BR, 64, 64), F32)],
        name="last",
    )(r, c_occupied, dens)


def solution(mesh):
    return jax.shard_map(
        on_device,
        mesh=mesh,
        in_specs=(P("ia", None, "ja"), P("ja", None, "ia"), P("ia"), P("ja"), P(), P(), P()),
        out_specs=(P("ia", "ja"), P("ia", "ja")),
        check_vma=False,
    )
```

time: 368 us -> 119 us (0.32)
  waiting for transfers between devices: 207 us -> 0 us
  Pallas kernels: 0 us -> 112 us
  blocking collectives: 42.9 us -> 0 us
  starting transfers between devices: 42.6 us -> 0 us
  local copies, waits for them, and re-layouts: 34.3 us -> 5.55 us
  between operations: 14.9 us -> 1.31 us
  other arithmetic: 11.6 us -> 0 us
  matrix products: 11.1 us -> 0 us
    reduce_scatter x1 -> x0, waiting for transfers between devices: 113 us -> none  [one_scatter(): lax.psum_scatter(lines, axis, tiled=True).reshape(-1)]
    pallas_call x0 -> x2, Pallas kernels: none -> 112 us  [the longest x1 108 us: on_device(): pl.pallas_call(main_kernel, out_shape=(jax.ShapeDtypeStruct((2, PLANE, 16...]
    all_gather x1 -> x0, waiting for transfers between devices: 65 us -> none  [stacked_from(): parts = lax.all_gather(parts, axes[k], axis=0, tiled=True)]
    all_gather x2 -> x0, blocking collectives: 42.9 us -> none  [stacked_from(): parts = lax.all_gather(parts, axes[k], axis=0, tiled=True)]
    all_to_all x3 -> x0, starting transfers between devices: 42.5 us -> none  [the longest x1 18.7 us: on_device(): lax.all_to_all(stacked, IA, split_axis=1, concat_axis=0, tiled=True)]
    all_to_all x3 -> x0, waiting for transfers between devices: 29.4 us -> none  [the longest x1 16.5 us: on_device(): lax.all_to_all(virtual_back, IA, split_axis=1, concat_axis=0, tiled=True)]
    reshape x4 -> x0, local copies, waits for them, and re-layouts: 12.8 us -> none  [the longest x2 7.24 us: one_scatter(): lines = jnp.concatenate([b.reshape(peers, -1) for b in parts], axis=1)]
    dot_general x5 -> x0, matrix products: 11.1 us -> none  [the longest x1 4.46 us: on_device(): jnp.einsum('iap,jbp->ijab', first_full, second_full, preferred_element_ty...]
  transfers between devices with their start and end apart: 5 -> 0, of which waited for: 4 -> 0; matrix products, arithmetic and copies ran while one was open for 3% -> 0% of each run, Pallas kernels for 0% -> 0%
where the time goes in v1:
time: 119 us
  Pallas kernels  112 us (94%)
  local copies, waits for them, and re-layouts  5.55 us (5%)
  between operations  1.31 us (1%)
    pallas_call x1, Pallas kernels, on_device(): pl.pallas_call(main_kernel, out_shape=(jax.ShapeDtypeStruct((2, PLANE, 16...  108 us
    unnamed x14, local copies, waits for them, and re-layouts  5.55 us
    pallas_call x1, Pallas kernels, on_device(): pl.pallas_call(last_kernel, out_shape=(jax.ShapeDtypeStruct((BR, 36864),...  4.32 us

profile of v1, /device:TPU:1, one launch (start us, length us, event | category | flops | bytes accessed | tf_op | source)
XLA Modules:
  0.0 119.1 jit_solution(13734401680036214678)
XLA Ops:
  1.3 0.0 copy-start
  1.3 1.3 %copy-done = f32[576,512]{1,0:T(8,128)S(1)} copy-done((f32[576,512]{1,0:T(8,128)S(1)}, f32[576,512]{1,0:T(8,128)}, u32[]{:S(2)}) %copy-start) | copy-done | bytes 1179672
  2.5 0.0 copy-start.2
  2.5 0.8 copy-done.2
  3.4 0.0 copy-start.3
  3.4 0.8 copy-done.3
  4.1 0.0 copy-start.5
  4.1 0.7 copy-done.5
  4.8 0.0 copy-start.6
  4.8 0.7 copy-done.6
  5.5 107.9 %pairs.1 = (f32[2,32,16,128]{3,2,1,0:T(8,128)S(1)}, f32[8,128]{1,0:T(8,128)S(1)}) custom-call(bf16[64,512]{1,0:T(8,128)(2,1)S(1)} %bitcast.7, bf16[2,16,512]{2,1,0:T(8,128)(2,1)S(1)} %bitcast.8, f32[1]{0:T(128)S(6)} %copy.9.e1, f32[2]{0:T(128)S(1)} %copy-done.6, f32[1,512]{1,0:T(1,128)S(1)} %bitcast.9, f32[8,72,512]{2,1,0:T(8,128)S(1)} %bitcast.6), custom_call_target="tpu_custom_call" | custom-call | tf_op jit(solution)/shard_map/pairs/pallas_call | solution.py:475
  113.4 0.0 copy-start.1
  113.4 0.8 copy-done.1
  114.2 0.0 copy-start.4
  114.2 0.6 copy-done.4
  114.8 4.3 %last.1 = (f32[9,36864]{1,0:T(8,128)}, f32[8,32]{1,0:T(8,128)}) custom-call(f32[2,32,16,128]{3,2,1,0:T(8,128)} %copy-done.1, f32[64,576]{1,0:T(8,128)} %co.1, f32[8,128]{1,0:T(8,128)} %copy-done.4), custom_call_target="tpu_custom_call" | custom-call | tf_op jit(solution)/shard_map/last/pallas_call | solution.py:516
Async XLA Ops:
  1.3 1.3 %copy-start = (f32[576,512]{1,0:T(8,128)S(1)}, f32[576,512]{1,0:T(8,128)}, u32[]{:S(2)}) copy-start(f32[576,512]{1,0:T(8,128)} %param.12) | copy-start | bytes 3538948
  2.5 0.8 copy-start.2
  3.4 0.8 copy-start.3
  4.1 0.7 copy-start.5
  4.8 0.7 copy-start.6
  113.4 0.8 copy-start.1
  114.2 0.6 copy-start.4

commit v2 on v1

--- a/solution.py
+++ b/solution.py
@@ -38,11 +38,12 @@
 
 
 def main_kernel(
-    bf, bs, e1, e2, ev, cv,
+    bf, bs, e1, e2, ev_hbm, cv_hbm,
     R, dens_out,
-    F, S, E, Chi, Clo, T, AR, Ghi, Glo, D, DP, DY, DX, DZ, DR, DO, QR, QL, SB,
+    ev, cv,
+    F, S, E, Chi, Clo, T, AR, G, D, DP, DY, DX, DZ, DR, DO, QR, QL, SB,
     f0_s, f0_r, fr_s, fr_r, fl_s, fl_r,
-    w_s, w_r, sx_s, sx_r, yr_s, yr_r, yl_s, yl_r, pc_s, pc_r, e_s, e_r,
+    w_s, w_r, xa_s, xa_r, xb_s, xb_r, ya_s, ya_r, yb_s, yb_r, pc_s, pc_r, e_s, e_r,
     qr_s, qr_r, ql_s, ql_r, dp_s, dp_r, dy_s, dy_r, dx_s, dx_r, dz_s, dz_r, do_s, do_r,
     a_s, a_r, r_s, r_r, loc,
 ):
@@ -58,6 +59,10 @@
     E[0, 0] = jnp.full((8, 128), e1[0], F32)
     E[0, 1] = jnp.full((8, 128), e2[0], F32)
     E[0, 2] = jnp.full((8, 128), e2[1], F32)
+    cv_in = pltpu.make_async_copy(cv_hbm, cv, loc.at[2])
+    ev_in = pltpu.make_async_copy(ev_hbm, ev, loc.at[3])
+    cv_in.start()
+    ev_in.start()
     barrier = pltpu.get_barrier_semaphore()
 
     def hail(to):
@@ -96,64 +101,81 @@
     e_far.start()
     e_mate.start()
 
-    def split_c(g):
-        hi, lo = split(cv[g])
-        Chi[g] = hi
-        Clo[g] = lo
-
-    pl.loop(0, 8)(split_c)
-
-    def x_sends(hp, slot):
-        for d in range(1, NX):
-            to = lax.rem(x + d, NX)
-            piece = S.at[c, x, hp, y]
-            remote(piece, piece, sx_s.at[slot, d - 1], sx_r.at[slot, d - 1], dev(to, y, z, c)).start()
-
-    def x_waits(hp, slot):
-        for d in range(1, NX):
-            frm = lax.rem(x + NX - d, NX)
-            piece = S.at[c, frm, hp, y]
-            remote(piece, piece, sx_s.at[slot, d - 1], sx_r.at[slot, d - 1], mate).wait_recv()
-        for d in range(1, NX):
-            piece = S.at[c, x, hp, y]
-            remote(piece, piece, sx_s.at[slot, d - 1], sx_r.at[slot, d - 1], mate).wait_send()
-
-    yr, yl = lax.rem(y + 1, NY), lax.rem(y + NY - 1, NY)
-
-    def y_block(hp, yo):
+    cv_in.wait()
+    ev_in.wait()
+    for hd in range(NH):
+        for q in range(2):
+            v = jnp.concatenate([cv[4 * q + hd], cv[4 * q + 2 + hd]], axis=0)
+            Chi[hd, q], Clo[hd, q] = split(v)
+
+    first = c == 0
+    ROWS = (4, 3, 5, 2, 6, 1, 7)
+    LINES = (2, 1, 3)
+
+    def piece(hp):
+        return S.at[c, x, hp, y]
+
+    def line(hp, xo):
+        return S.at[c, xo, hp]
+
+    def column(hp, yo):
         return S.at[c, :, hp, yo]
 
-    def y_copy(hp, slot, s, right):
-        yo = lax.rem(y + NY - s, NY) if right else lax.rem(y + s, NY)
-        b = y_block(hp, yo)
-        ss, rs = (yr_s, yr_r) if right else (yl_s, yl_r)
-        return remote(b, b, ss.at[slot, s], rs.at[slot, s], dev(x, yr if right else yl, z, c))
-
-    def y_got(hp, slot, s, right):
-        yo = lax.rem(y + NY - s, NY) if right else lax.rem(y + s, NY)
-        b = y_block(hp, yo)
-        ss, rs = (yr_s, yr_r) if right else (yl_s, yl_r)
-        remote(b, b, ss.at[slot, s - 1], rs.at[slot, s - 1], mate).wait_recv()
-
-    def share(hp, slot, n, yo):
-        b = y_block(hp, yo)
-        remote(b, b, pc_s.at[slot, n], pc_r.at[slot, n], mate).start()
-
-    def y_step(hp, slot, s):
-        if s == 0:
-            y_copy(hp, slot, 0, True).start()
-            y_copy(hp, slot, 0, False).start()
-            share(hp, slot, 0, y)
-            return
-        y_got(hp, slot, s, True)
-        if s < 4:
-            y_copy(hp, slot, s, True).start()
-        share(hp, slot, s, lax.rem(y + NY - s, NY))
-        if s < 4:
-            y_got(hp, slot, s, False)
-            if s < 3:
-                y_copy(hp, slot, s, False).start()
-            share(hp, slot, 4 + s, lax.rem(y + s, NY))
+    def along_y(ref, to, slot, d, stage):
+        ss, rs = (ya_s, ya_r) if stage == 1 else (yb_s, yb_r)
+        return remote(ref, ref, ss.at[slot, d], rs.at[slot, d], dev(x, to, z, c))
+
+    def along_x(ref, to, slot, d, stage):
+        ss, rs = (xa_s, xa_r) if stage == 1 else (xb_s, xb_r)
+        return remote(ref, ref, ss.at[slot, d], rs.at[slot, d], dev(to, y, z, c))
+
+    def share(ref, slot, n):
+        remote(ref, ref, pc_s.at[slot, n], pc_r.at[slot, n], mate).start()
+
+    def stage_1(hp, slot):
+        @pl.when(first)
+        def _():
+            for d in ROWS:
+                along_y(piece(hp), lax.rem(y + d, NY), slot, d, 1).start()
+
+        @pl.when(jnp.logical_not(first))
+        def _():
+            for d in LINES:
+                along_x(piece(hp), lax.rem(x + d, NX), slot, d, 1).start()
+
+    def stage_2(hp, slot):
+        @pl.when(first)
+        def _():
+            for d in ROWS:
+                along_y(S.at[c, x, hp, lax.rem(y + NY - d, NY)], yr, slot, d, 1).wait_recv()
+            for d in LINES:
+                along_x(line(hp, x), lax.rem(x + d, NX), slot, d, 2).start()
+            share(line(hp, x), slot, 0)
+
+        @pl.when(jnp.logical_not(first))
+        def _():
+            for d in LINES:
+                along_x(S.at[c, lax.rem(x + NX - d, NX), hp, y], lax.rem(x + 1, NX), slot, d, 1).wait_recv()
+            for d in ROWS:
+                along_y(column(hp, y), lax.rem(y + d, NY), slot, d, 2).start()
+            share(column(hp, y), slot, 0)
+
+    def stage_3(hp, slot, lines, rows):
+        @pl.when(first)
+        def _():
+            for d in lines:
+                b = line(hp, lax.rem(x + NX - d, NX))
+                along_x(b, lax.rem(x + 1, NX), slot, d, 2).wait_recv()
+                share(b, slot, d)
+
+        @pl.when(jnp.logical_not(first))
+        def _():
+            for d in rows:
+                b = column(hp, lax.rem(y + NY - d, NY))
+                along_y(b, yr, slot, d, 2).wait_recv()
+                share(b, slot, d)
+
+    yr = lax.rem(y + 1, NY)
 
     zr, zl = lax.rem(z + 1, NZ), lax.rem(z + NZ - 1, NZ)
 
@@ -168,8 +190,8 @@
 
             @pl.when(o // 8 == c)
             def _():
-                for q in range(2):
-                    b = F.at[lax.rem(o, NL) * 2 + q]
+                for q in range(4):
+                    b = F.at[lax.rem(o, NL) * 2 + q // 2, pl.ds(q % 2 * 32, 32)]
                     if s > 0:
                         remote(b, b, ss.at[s - 1, q], rs.at[s - 1, q], to).wait_recv()
                     if s < last:
@@ -186,37 +208,39 @@
         remote(bs.at[c], S.at[c, x, h, y], w_s.at[0], w_r.at[0], mate).wait_recv()
 
     other = 1 - h
-    x_sends(h, 0)
+    stage_1(h, 0)
     f_step(0)
-    x_waits(h, 0)
-    y_step(h, 0, 0)
     f_step(1)
-    y_step(h, 0, 1)
+    stage_2(h, 0)
     f_step(2)
-    y_step(h, 0, 2)
     remote(bs.at[c], S.at[c, x, other, y], w_s.at[0], w_r.at[1], mate).wait_recv()
-    x_sends(other, 1)
+    stage_1(other, 1)
     f_step(3)
-    y_step(h, 0, 3)
-    x_waits(other, 1)
-    y_step(other, 1, 0)
     f_step(4)
-    y_step(h, 0, 4)
-    y_step(other, 1, 1)
+    stage_2(other, 1)
     f_step(5)
-    y_step(other, 1, 2)
+    stage_3(h, 0, LINES, ROWS)
     f_step(6)
-    y_step(other, 1, 3)
     f_step(7)
-    y_step(other, 1, 4)
+    stage_3(other, 1, LINES[:1], ROWS[:3])
     f_step(8)
+    stage_3(other, 1, LINES[1:], ROWS[3:])
 
     e_far.wait()
     e_mate.wait()
     for slot, hp in ((0, h), (1, other)):
-        for n in range(NY):
-            b = S.at[k, :, hp, n]
-            remote(b, b, pc_s.at[slot, n], pc_r.at[slot, n], mate).wait_recv()
+
+        @pl.when(first)
+        def _():
+            for n in range(NY):
+                b = S.at[k, :, hp, lax.rem(y + NY - n, NY)]
+                remote(b, b, pc_s.at[slot, n], pc_r.at[slot, n], mate).wait_recv()
+
+        @pl.when(jnp.logical_not(first))
+        def _():
+            for n in range(NX):
+                b = S.at[k, lax.rem(x + NX - n, NX), hp]
+                remote(b, b, pc_s.at[slot, n], pc_r.at[slot, n], mate).wait_recv()
 
     ei = jnp.where(home, E[0, 0, 0:1, 0:1], E[1, 0, 0:1, 0:1])
     row = ev[...]
@@ -246,17 +270,14 @@
         acc = dot(T[0], S[0, gx, gh].reshape(128, 512), 1, 1)
         acc += dot(T[1], S[1, gx, gh].reshape(128, 512), 1, 1)
         hi, lo = split(acc)
-        Ghi[g] = hi
-        Glo[g] = lo
-
-    def own(d, q):
+        G[g, :, 0:128] = hi
+        G[g, :, 128:256] = lo
+
+    def own(d):
         hd, ld = d // 8, d % 8
-        ghi, glo = Ghi[ld], Glo[ld]
-        out = []
-        for xi in (2 * q, 2 * q + 1):
-            chi, clo = Chi[xi * 2 + hd], Clo[xi * 2 + hd]
-            out.append(dot(chi, ghi, 1, 0) + dot(clo, ghi, 1, 0) + dot(chi, glo, 1, 0))
-        return jnp.concatenate(out, axis=0)
+        both = dot(Chi[hd].reshape(288, 512), G[ld], 1, 0)
+        out = both[:, 0:128] + both[:, 128:256] + dot(Clo[hd].reshape(288, 512), G[ld, :, 0:128], 1, 0)
+        return out[0:144], out[144:288]
 
     def q_copy(buf, s, q, right):
         ss, rs = (qr_s, qr_r) if right else (ql_s, ql_r)
@@ -266,8 +287,9 @@
 
     for right, buf in ((True, QR), (False, QL)):
         d0 = lax.rem(z + (8 if right else 9), NZ)
+        mine = own(d0)
         for q in range(2):
-            buf[0, q] = own(d0, q)
+            buf[0, q] = mine[q]
             q_copy(buf, 0, q, right).start()
 
     def q_steps(lo, hi):
@@ -276,10 +298,10 @@
             dr = lax.rem(z + 8 + NZ - s, NZ)
             dl = lax.rem(z + 9 + s, NZ)
             for right, buf, d in ((True, QR, dr), (False, QL, dl)):
+                mine = own(d)
                 for q in range(2):
-                    mine = own(d, q)
                     q_copy(buf, s - 1, q, right).wait_recv()
-                    buf[s, q] += mine
+                    buf[s, q] += mine[q]
                     q_copy(buf, s, q, right).start()
 
     for t in range(4):
@@ -337,20 +359,20 @@
             ).start()
 
     q_steps(6, 7)
+    mine = own(lax.rem(z + 1, NZ))
     for q in range(2):
-        mine = own(lax.rem(z + 1, NZ), q)
         q_copy(QR, 6, q, True).wait_recv()
-        QR[7, q] += mine
+        QR[7, q] += mine[q]
         q_copy(QR, 7, q, True).start()
+    mine = own(z)
     for q in range(2):
-        mine = own(z, q)
         q_copy(QL, 6, q, False).wait_recv()
-        QL[7, q] += mine
+        QL[7, q] += mine[q]
     for q in range(2):
         q_copy(QR, 7, q, True).wait_recv()
         got = QR[8, q] + QL[7, q]
         for i in range(16):
-            SB[q * 16 + i, 0:BR] = got[i * BR : i * BR + BR]
+            SB[q * 16 + i] = got[i * BR : i * BR + BR]
         for i in range(16):
             b = q * 16 + i
 
@@ -369,13 +391,21 @@
         DO[...] = tile
         remote(DO, DO, do_s, do_r, mate).start()
 
-    @pl.loop(1, PLANE)
-    def _(d):
-        b = lax.rem(ip + d, PLANE)
-        remote(SB.at[b], R.at[c, b], a_s.at[b], a_r.at[b], mate).wait_recv()
-
-    half = remote(R.at[c], R.at[c], r_s, r_r, mate)
-    half.start()
+    def group(core, d):
+        b = R.at[core, pl.ds(lax.rem(x + d, NX) * NY, NY)]
+        return remote(b, b, r_s.at[d], r_r.at[d], mate)
+
+    for d in (0, 1, 3, 2):
+
+        @pl.loop(0, NY)
+        def _(yy):
+            b = lax.rem(x + d, NX) * NY + yy
+
+            @pl.when(b != ip)
+            def _():
+                remote(SB.at[b], R.at[c, b], a_s.at[b], a_r.at[b], mate).wait_recv()
+
+        group(c, d).start()
 
     @pl.when(jnp.logical_not(act))
     def _():
@@ -400,18 +430,30 @@
 
             @pl.when(o // 8 == c)
             def _():
-                for q in range(2):
-                    b = F.at[lax.rem(o, NL) * 2 + q]
+                for q in range(4):
+                    b = F.at[lax.rem(o, NL) * 2 + q // 2, pl.ds(q % 2 * 32, 32)]
                     remote(b, b, ss.at[s, q], fr_r.at[s, q], mate).wait_send()
 
     for slot in range(2):
-        for s in range(4):
-            y_copy(h, slot, s, True).wait_send()
-            if s < 3:
-                y_copy(h, slot, s, False).wait_send()
-        for n in range(NY):
-            b = y_block(h, 0)
-            remote(b, b, pc_s.at[slot, n], pc_r.at[slot, n], mate).wait_send()
+
+        @pl.when(first)
+        def _():
+            for d in ROWS:
+                along_y(piece(h), yr, slot, d, 1).wait_send()
+            for d in LINES:
+                along_x(line(h, x), lax.rem(x + 1, NX), slot, d, 2).wait_send()
+            for n in range(NX):
+                remote(line(h, x), line(h, x), pc_s.at[slot, n], pc_r.at[slot, n], mate).wait_send()
+
+        @pl.when(jnp.logical_not(first))
+        def _():
+            for d in LINES:
+                along_x(piece(h), lax.rem(x + 1, NX), slot, d, 1).wait_send()
+            for d in ROWS:
+                along_y(column(h, y), yr, slot, d, 2).wait_send()
+            for n in range(NY):
+                remote(column(h, y), column(h, y), pc_s.at[slot, n], pc_r.at[slot, n], mate).wait_send()
+
     for s in range(8):
         for q in range(2):
             q_copy(QR, s, q, True).wait_send()
@@ -437,13 +479,17 @@
         b = lax.rem(ip + d, PLANE)
         remote(SB.at[b], R.at[c, b], a_s.at[b], a_r.at[b], mate).wait_send()
 
-    half.wait_send()
-    remote(R.at[k], R.at[k], r_s, r_r, mate).wait_recv()
-
-
-def last_kernel(r, co, dens, gamma, density, W, L):
+    for d in range(NX):
+        group(c, d).wait_send()
+        group(k, d).wait_recv()
+
+
+def last_kernel(r, co_hbm, dens, gamma_hbm, density, co, gamma, W, LT, L, sem, out_sem):
     _, _, _, l, c = place()
+    co_in = pltpu.make_async_copy(co_hbm, co, sem)
+    co_in.start()
     W[...] = jnp.zeros_like(W)
+    co_in.wait()
     for hi in range(2):
         for x in range(NX):
             rows = co[(x * 2 + hi) * 8 : (x * 2 + hi) * 8 + 8, :]
@@ -452,18 +498,25 @@
             W[64 + at : 64 + at + 8, 576:1152] = rows
     w_hi, w_lo = split(W[...])
     for n in range(BR):
-        both = jnp.transpose(r[:, :, n, :].reshape(64, 128))
-        L[0, n], L[1, n] = both[0:64], both[64:128]
-    for n in range(BR):
-        even = L[c, n, pl.ds(0, 32, stride=2), :]
-        odd = L[c, n, pl.ds(1, 32, stride=2), :]
-        l_hi, l_lo = split(jnp.concatenate([even, odd], axis=1))
+        LT[n] = jnp.transpose(r[:, :, n, :].reshape(64, 128))
+        even = LT[n, pl.ds(c * 64, 32, stride=2), :]
+        odd = LT[n, pl.ds(c * 64 + 1, 32, stride=2), :]
+        L[pl.ds(n, 32, stride=16), :] = jnp.concatenate([even, odd], axis=1)
+    outs = []
+    for g in range(4):
+        l_hi, l_lo = split(L[g * 128 : g * 128 + 128, :])
         res = dot(l_hi, w_hi, 1, 0) + dot(l_lo, w_hi, 1, 0) + dot(l_hi, w_lo, 1, 0)
-        for t in range(32):
-            gamma[n : n + 1, t * 1152 : t * 1152 + 1152] = res[t : t + 1, :]
+        for t in range(8):
+            at = (g * 8 + t) * 1152
+            gamma[:, at : at + 1152] = res[t * 16 : t * 16 + BR, :]
+        cols = pl.ds(g * 9216, 9216)
+        outs.append(pltpu.make_async_copy(gamma.at[:, cols], gamma_hbm.at[:, cols], out_sem.at[g]))
+        outs[-1].start()
     at = (l % 2) * 64 + c * 32
     turned = pltpu.roll(dens[...], lax.rem(128 - at, 128), 1)
     density[...] = turned[:, 0:32] * (1.0 / 2048.0)
+    for copy in outs:
+        copy.wait()
 
 
 def on_device(b_first, b_second, eps_first, eps_second, eps_virtual, c_virtual, c_occupied):
@@ -472,24 +525,26 @@
     dma = pltpu.SemaphoreType.DMA
     vm = pl.BlockSpec(memory_space=pltpu.VMEM)
     sm = pl.BlockSpec(memory_space=pltpu.SMEM)
+    hb = pl.BlockSpec(memory_space=pltpu.HBM)
     r, dens = pl.pallas_call(
         main_kernel,
         out_shape=(
-            jax.ShapeDtypeStruct((2, PLANE, 16, 128), F32),
+            jax.ShapeDtypeStruct((2, PLANE, BR, 128), F32),
             jax.ShapeDtypeStruct((8, 128), F32),
         ),
-        in_specs=[vm, vm, sm, sm, vm, vm],
+        in_specs=[hb, hb, sm, sm, hb, hb],
         out_specs=(vm, vm),
         scratch_shapes=[
+            pltpu.VMEM((1, 512), F32),
+            pltpu.VMEM((8, CR, 512), F32),
             pltpu.VMEM((16, 64, 512), BF16),
             pltpu.VMEM((2, NX, NH, NY, 16, 512), BF16),
             pltpu.VMEM((3, 3, 8, 128), F32),
-            pltpu.VMEM((8, CR, 512), BF16),
-            pltpu.VMEM((8, CR, 512), BF16),
+            pltpu.VMEM((NH, 2, 144, 512), BF16),
+            pltpu.VMEM((NH, 2, 144, 512), BF16),
             pltpu.VMEM((2, 512, 512), BF16),
             pltpu.VMEM((2, 512, 512), BF16),
-            pltpu.VMEM((8, 512, 128), BF16),
-            pltpu.VMEM((8, 512, 128), BF16),
+            pltpu.VMEM((8, 512, 256), BF16),
             pltpu.VMEM((2, 4, 8, 8, 512), F32),
             pltpu.VMEM((4, 8, 8, 512), F32),
             pltpu.VMEM((7, 4, 8, 512), F32),
@@ -499,17 +554,17 @@
             pltpu.VMEM((8, 128), F32),
             pltpu.VMEM((9, 2, 144, 128), F32),
             pltpu.VMEM((8, 2, 144, 128), F32),
-            pltpu.VMEM((PLANE, 16, 128), F32),
-            dma, dma, dma((8, 2)), dma((8, 2)), dma((7, 2)), dma((7, 2)),
-            dma((2,)), dma((2,)), dma((2, 3)), dma((2, 3)),
-            dma((2, 4)), dma((2, 4)), dma((2, 3)), dma((2, 3)), dma((2, 8)), dma((2, 8)),
+            pltpu.VMEM((PLANE, BR, 128), F32),
+            dma, dma, dma((8, 4)), dma((8, 4)), dma((7, 4)), dma((7, 4)),
+            dma((2,)), dma((2,)), dma((2, 4)), dma((2, 4)), dma((2, 4)), dma((2, 4)),
+            dma((2, 8)), dma((2, 8)), dma((2, 8)), dma((2, 8)), dma((2, 8)), dma((2, 8)),
             dma((2,)), dma((2,)),
             dma((8, 2)), dma((8, 2)), dma((7, 2)), dma((7, 2)), dma, dma, dma((7,)), dma((7,)),
             dma((2,)), dma((4,)), dma((16,)), dma((16,)), dma, dma,
-            dma((PLANE,)), dma((PLANE,)), dma, dma, dma((2,)),
+            dma((PLANE,)), dma((PLANE,)), dma((NX,)), dma((NX,)), dma((4,)),
         ],
         compiler_params=pltpu.CompilerParams(
-            collective_id=0, has_side_effects=True, vmem_limit_bytes=48 << 20
+            collective_id=0, has_side_effects=True, vmem_limit_bytes=66_560_000
         ),
         name="pairs",
     )(bf, bs, eps_first, eps_second, eps_virtual.reshape(1, 512), c_virtual.reshape(8, CR, 512))
@@ -519,9 +574,18 @@
             jax.ShapeDtypeStruct((BR, 36864), F32),
             jax.ShapeDtypeStruct((8, 32), F32),
         ),
-        in_specs=[vm, vm, vm],
-        out_specs=(vm, vm),
-        scratch_shapes=[pltpu.VMEM((128, 1152), F32), pltpu.VMEM((2, BR, 64, 64), F32)],
+        in_specs=[vm, hb, vm],
+        out_specs=(hb, vm),
+        scratch_shapes=[
+            pltpu.VMEM((64, 576), F32),
+            pltpu.VMEM((BR, 36864), F32),
+            pltpu.VMEM((128, 1152), F32),
+            pltpu.VMEM((BR, 128, 64), F32),
+            pltpu.VMEM((512, 128), F32),
+            dma,
+            dma((4,)),
+        ],
+        compiler_params=pltpu.CompilerParams(vmem_limit_bytes=66_560_000),
         name="last",
     )(r, c_occupied, dens)
 

time: 119 us -> 114 us (0.958)
  local copies, waits for them, and re-layouts: 5.55 us -> 0 us
    unnamed x14 -> x0, local copies, waits for them, and re-layouts: 5.55 us -> none
where the time goes in v2:
time: 114 us
  Pallas kernels  112 us (98%)
  between operations  1.28 us (1%)
    pallas_call x1, Pallas kernels, on_device(): pl.pallas_call(main_kernel, out_shape=(jax.ShapeDtypeStruct((2, PLANE, BR...  107 us
    pallas_call x1, Pallas kernels, on_device(): pl.pallas_call(last_kernel, out_shape=(jax.ShapeDtypeStruct((BR, 36864),...  5.05 us

profile of v2, /device:TPU:1, one launch (start us, length us, event | category | flops | bytes accessed | tf_op | source)
XLA Modules:
  0.0 113.6 jit_solution(13353202394580863537)
XLA Ops:
  1.3 107.2 %pairs.1 = (f32[2,32,9,128]{3,2,1,0:T(8,128)}, f32[8,128]{1,0:T(8,128)}) custom-call(bf16[64,512]{1,0:T(8,128)(2,1)} %bitcast.7, bf16[2,16,512]{2,1,0:T(8,128)(2,1)} %bitcast.8, f32[1]{0:T(128)S(6)} %copy.9.e1, f32[2]{0:T(128)} %e2.1, f32[1,512]{1,0:T(1,128)} %bitcast.9, f32[8,72,512]{2,1,0:T(8,128)} %bitcast.6), custom_call_target="tpu_custom_call" | custom-call | tf_op jit(solution)/shard_map/pairs/pallas_call | solution.py:529
  108.5 5.1 %last.1 = (f32[9,36864]{1,0:T(8,128)}, f32[8,32]{1,0:T(8,128)}) custom-call(f32[2,32,9,128]{3,2,1,0:T(8,128)} %get-tuple-element.4.r, f32[64,576]{1,0:T(8,128)} %co_hbm.1, f32[8,128]{1,0:T(8,128)} %get-tuple-element.5.dens), custom_call_target="tpu_custom_call" | custom-call | tf_op jit(solution)/shard_map/last/pallas_call | solution.py:571

commit v3 on v2

--- a/solution.py
+++ b/solution.py
@@ -41,7 +41,7 @@
     bf, bs, e1, e2, ev_hbm, cv_hbm,
     R, dens_out,
     ev, cv,
-    F, S, E, Chi, Clo, T, AR, G, D, DP, DY, DX, DZ, DR, DO, QR, QL, SB,
+    F, S, E, Chi, Clo, T, AR, G32, G, D, DP, DY, DX, DZ, DR, DO, QR, QL, SB,
     f0_s, f0_r, fr_s, fr_r, fl_s, fl_r,
     w_s, w_r, xa_s, xa_r, xb_s, xb_r, ya_s, ya_r, yb_s, yb_r, pc_s, pc_r, e_s, e_r,
     qr_s, qr_r, ql_s, ql_r, dp_s, dp_r, dy_s, dy_r, dx_s, dx_r, dz_s, dz_r, do_s, do_r,
@@ -228,23 +228,10 @@
 
     e_far.wait()
     e_mate.wait()
-    for slot, hp in ((0, h), (1, other)):
-
-        @pl.when(first)
-        def _():
-            for n in range(NY):
-                b = S.at[k, :, hp, lax.rem(y + NY - n, NY)]
-                remote(b, b, pc_s.at[slot, n], pc_r.at[slot, n], mate).wait_recv()
-
-        @pl.when(jnp.logical_not(first))
-        def _():
-            for n in range(NX):
-                b = S.at[k, lax.rem(x + NX - n, NX), hp]
-                remote(b, b, pc_s.at[slot, n], pc_r.at[slot, n], mate).wait_recv()
-
     ei = jnp.where(home, E[0, 0, 0:1, 0:1], E[1, 0, 0:1, 0:1])
     row = ev[...]
-    for j in range(2):
+
+    def amplitude(j):
         ej = jnp.where(home, E[0, 1 + j, 0:1, 0:1], E[2, 1 + j, 0:1, 0:1])
 
         @pl.loop(0, 4)
@@ -260,16 +247,38 @@
             r = 1.0 / (ei + ej - (col + row))
             a = i_ab * r
             at = i_ba * r
-            rows = pl.ds(pl.multiple_of(t * 128, 128), 128)
-            T[j, rows, :] = (2.0 * a - at).astype(BF16)
-            AR[j, rows, :] = at.astype(BF16)
+            T[j, cols, :] = (2.0 * a - at).astype(BF16)
+            AR[j, cols, :] = at.astype(BF16)
+
+    amplitude(c)
 
     @pl.loop(0, 8)
     def _(g):
-        gx, gh = g // 2, g % 2
-        acc = dot(T[0], S[0, gx, gh].reshape(128, 512), 1, 1)
-        acc += dot(T[1], S[1, gx, gh].reshape(128, 512), 1, 1)
-        hi, lo = split(acc)
+        G32[g] = dot(T[c], S[c, g // 2, g % 2].reshape(128, 512), 1, 1)
+
+    for t in range(4):
+        acc = dot(T[c, t * 128 : t * 128 + 128, :], AR[c], 1, 0)
+        D[t // 2, (t % 2) * 2 : (t % 2) * 2 + 2] = acc.reshape(2, 8, 8, 512)
+
+    for slot, hp in ((0, h), (1, other)):
+
+        @pl.when(first)
+        def _():
+            for n in range(NY):
+                b = S.at[k, :, hp, lax.rem(y + NY - n, NY)]
+                remote(b, b, pc_s.at[slot, n], pc_r.at[slot, n], mate).wait_recv()
+
+        @pl.when(jnp.logical_not(first))
+        def _():
+            for n in range(NX):
+                b = S.at[k, lax.rem(x + NX - n, NX), hp]
+                remote(b, b, pc_s.at[slot, n], pc_r.at[slot, n], mate).wait_recv()
+
+    amplitude(k)
+
+    @pl.loop(0, 8)
+    def _(g):
+        hi, lo = split(G32[g] + dot(T[k], S[k, g // 2, g % 2].reshape(128, 512), 1, 1))
         G[g, :, 0:128] = hi
         G[g, :, 128:256] = lo
 
@@ -277,7 +286,7 @@
         hd, ld = d // 8, d % 8
         both = dot(Chi[hd].reshape(288, 512), G[ld], 1, 0)
         out = both[:, 0:128] + both[:, 128:256] + dot(Clo[hd].reshape(288, 512), G[ld, :, 0:128], 1, 0)
-        return out[0:144], out[144:288]
+        return [out[q * CR : q * CR + CR] for q in range(4)]
 
     def q_copy(buf, s, q, right):
         ss, rs = (qr_s, qr_r) if right else (ql_s, ql_r)
@@ -285,33 +294,42 @@
             buf.at[s, q], buf.at[s + 1, q], ss.at[s, q], rs.at[s, q], dev(x, y, zr if right else zl, c)
         )
 
+    EARLY = {True: (0, 1), False: (2, 3)}
+    LATE = {True: (2, 3), False: (0, 1)}
+    mine = own(lax.rem(z + 8, NZ))
     for right, buf in ((True, QR), (False, QL)):
-        d0 = lax.rem(z + (8 if right else 9), NZ)
-        mine = own(d0)
-        for q in range(2):
+        for q in EARLY[right]:
             buf[0, q] = mine[q]
             q_copy(buf, 0, q, right).start()
+    for right, buf in ((True, QR), (False, QL)):
+        mine = own(lax.rem(z + (7 if right else 9), NZ))
+        for q in LATE[right]:
+            buf[1, q] = mine[q]
+            q_copy(buf, 1, q, right).start()
+        for q in EARLY[right]:
+            q_copy(buf, 0, q, right).wait_recv()
+            buf[1, q] += mine[q]
+            q_copy(buf, 1, q, right).start()
 
     def q_steps(lo, hi):
         @pl.loop(lo, hi)
         def _(s):
             dr = lax.rem(z + 8 + NZ - s, NZ)
-            dl = lax.rem(z + 9 + s, NZ)
+            dl = lax.rem(z + 8 + s, NZ)
             for right, buf, d in ((True, QR, dr), (False, QL, dl)):
                 mine = own(d)
-                for q in range(2):
+                for q in (*EARLY[right], *LATE[right]):
                     q_copy(buf, s - 1, q, right).wait_recv()
                     buf[s, q] += mine[q]
                     q_copy(buf, s, q, right).start()
 
     for t in range(4):
-        acc = dot(T[0, t * 128 : t * 128 + 128, :], AR[0], 1, 0)
-        acc += dot(T[1, t * 128 : t * 128 + 128, :], AR[1], 1, 0)
-        D[t // 2, (t % 2) * 2 : (t % 2) * 2 + 2] = acc.reshape(2, 8, 8, 512)
+        acc = dot(T[k, t * 128 : t * 128 + 128, :], AR[k], 1, 0)
+        D[t // 2, (t % 2) * 2 : (t % 2) * 2 + 2] += acc.reshape(2, 8, 8, 512)
     d_mate = remote(D.at[k], DP, dp_s, dp_r, mate)
     d_mate.start()
 
-    q_steps(1, 2)
+    q_steps(2, 3)
 
     d_mate.wait_recv()
 
@@ -323,7 +341,7 @@
         to = lax.rem(y + d, NY)
         remote(D.at[c, :, to], DY.at[d - 1], dy_s.at[d - 1], dy_r.at[d - 1], dev(x, to, z, c)).start()
 
-    q_steps(2, 5)
+    q_steps(3, 6)
 
     total = D[c, :, y]
     for d in range(1, NY):
@@ -340,7 +358,7 @@
             slot = lax.rem(x + NX - to, NX)
             remote(DX.at[0, i], DX.at[slot, 0], dx_s.at[i], dx_r.at[slot], dev(to, y, z, c)).start()
 
-    q_steps(5, 6)
+    q_steps(6, 7)
 
     @pl.when(act)
     def _():
@@ -358,23 +376,16 @@
                 DZ.at[zt // 8, (zt % 8) // 2], DR.at[d], dz_s.at[d], dz_r.at[d], dev(x, y, zt, c)
             ).start()
 
-    q_steps(6, 7)
-    mine = own(lax.rem(z + 1, NZ))
-    for q in range(2):
-        q_copy(QR, 6, q, True).wait_recv()
-        QR[7, q] += mine[q]
-        q_copy(QR, 7, q, True).start()
+    q_steps(7, 8)
     mine = own(z)
-    for q in range(2):
-        q_copy(QL, 6, q, False).wait_recv()
-        QL[7, q] += mine[q]
-    for q in range(2):
+    for q in range(4):
         q_copy(QR, 7, q, True).wait_recv()
-        got = QR[8, q] + QL[7, q]
-        for i in range(16):
-            SB[q * 16 + i] = got[i * BR : i * BR + BR]
-        for i in range(16):
-            b = q * 16 + i
+        q_copy(QL, 7, q, False).wait_recv()
+        got = QR[8, q] + QL[8, q] + mine[q]
+        for i in range(NY):
+            SB[q * NY + i] = got[i * BR : i * BR + BR]
+        for i in range(NY):
+            b = q * NY + i
 
             @pl.when(b != ip)
             def _():
@@ -454,11 +465,10 @@
             for n in range(NY):
                 remote(column(h, y), column(h, y), pc_s.at[slot, n], pc_r.at[slot, n], mate).wait_send()
 
-    for s in range(8):
-        for q in range(2):
-            q_copy(QR, s, q, True).wait_send()
-            if s < 7:
-                q_copy(QL, s, q, False).wait_send()
+    for right, buf in ((True, QR), (False, QL)):
+        for s in range(8):
+            for q in EARLY[right] if s == 0 else range(4):
+                q_copy(buf, s, q, right).wait_send()
     d_mate.wait_send()
     for d in range(1, NY):
         remote(D.at[c, :, 0], DY.at[d - 1], dy_s.at[d - 1], dy_r.at[d - 1], mate).wait_send()
@@ -484,10 +494,12 @@
         group(k, d).wait_recv()
 
 
-def last_kernel(r, co_hbm, dens, gamma_hbm, density, co, gamma, W, LT, L, sem, out_sem):
+def last_kernel(r_hbm, co_hbm, dens, gamma_hbm, density, r, co, gamma, W, LT, L, sem, out_sem):
     _, _, _, l, c = place()
-    co_in = pltpu.make_async_copy(co_hbm, co, sem)
+    co_in = pltpu.make_async_copy(co_hbm, co, sem.at[0])
+    r_in = pltpu.make_async_copy(r_hbm, r, sem.at[1])
     co_in.start()
+    r_in.start()
     W[...] = jnp.zeros_like(W)
     co_in.wait()
     for hi in range(2):
@@ -497,6 +509,7 @@
             W[at : at + 8, 0:576] = rows
             W[64 + at : 64 + at + 8, 576:1152] = rows
     w_hi, w_lo = split(W[...])
+    r_in.wait()
     for n in range(BR):
         LT[n] = jnp.transpose(r[:, :, n, :].reshape(64, 128))
         even = LT[n, pl.ds(c * 64, 32, stride=2), :]
@@ -544,6 +557,7 @@
             pltpu.VMEM((NH, 2, 144, 512), BF16),
             pltpu.VMEM((2, 512, 512), BF16),
             pltpu.VMEM((2, 512, 512), BF16),
+            pltpu.VMEM((8, 512, 128), F32),
             pltpu.VMEM((8, 512, 256), BF16),
             pltpu.VMEM((2, 4, 8, 8, 512), F32),
             pltpu.VMEM((4, 8, 8, 512), F32),
@@ -552,14 +566,14 @@
             pltpu.VMEM((2, 4, 8, 128), F32),
             pltpu.VMEM((16, 8, 128), F32),
             pltpu.VMEM((8, 128), F32),
-            pltpu.VMEM((9, 2, 144, 128), F32),
-            pltpu.VMEM((8, 2, 144, 128), F32),
+            pltpu.VMEM((9, 4, CR, 128), F32),
+            pltpu.VMEM((9, 4, CR, 128), F32),
             pltpu.VMEM((PLANE, BR, 128), F32),
             dma, dma, dma((8, 4)), dma((8, 4)), dma((7, 4)), dma((7, 4)),
             dma((2,)), dma((2,)), dma((2, 4)), dma((2, 4)), dma((2, 4)), dma((2, 4)),
             dma((2, 8)), dma((2, 8)), dma((2, 8)), dma((2, 8)), dma((2, 8)), dma((2, 8)),
             dma((2,)), dma((2,)),
-            dma((8, 2)), dma((8, 2)), dma((7, 2)), dma((7, 2)), dma, dma, dma((7,)), dma((7,)),
+            dma((8, 4)), dma((8, 4)), dma((8, 4)), dma((8, 4)), dma, dma, dma((7,)), dma((7,)),
             dma((2,)), dma((4,)), dma((16,)), dma((16,)), dma, dma,
             dma((PLANE,)), dma((PLANE,)), dma((NX,)), dma((NX,)), dma((4,)),
         ],
@@ -574,15 +588,16 @@
             jax.ShapeDtypeStruct((BR, 36864), F32),
             jax.ShapeDtypeStruct((8, 32), F32),
         ),
-        in_specs=[vm, hb, vm],
+        in_specs=[hb, hb, vm],
         out_specs=(hb, vm),
         scratch_shapes=[
+            pltpu.VMEM((2, PLANE, BR, 128), F32),
             pltpu.VMEM((64, 576), F32),
             pltpu.VMEM((BR, 36864), F32),
             pltpu.VMEM((128, 1152), F32),
             pltpu.VMEM((BR, 128, 64), F32),
             pltpu.VMEM((512, 128), F32),
-            dma,
+            dma((2,)),
             dma((4,)),
         ],
         compiler_params=pltpu.CompilerParams(vmem_limit_bytes=66_560_000),

time: 114 us -> 115 us (level)
    pallas_call x1, Pallas kernels: 107 us -> 109 us  [on_device(): pl.pallas_call(main_kernel, out_shape=(jax.ShapeDtypeStruct((2, PLANE, BR...]
where the time goes in v3:
time: 115 us
  Pallas kernels  113 us (98%)
  between operations  1.28 us (1%)
    pallas_call x1, Pallas kernels, on_device(): pl.pallas_call(main_kernel, out_shape=(jax.ShapeDtypeStruct((2, PLANE, BR...  109 us
    pallas_call x1, Pallas kernels, on_device(): pl.pallas_call(last_kernel, out_shape=(jax.ShapeDtypeStruct((BR, 36864),...  4.83 us

profile of v3, /device:TPU:1, one launch (start us, length us, event | category | flops | bytes accessed | tf_op | source)
XLA Modules:
  0.0 114.6 jit_solution(18250034168468755941)
XLA Ops:
  1.3 108.5 %pairs.1 = (f32[2,32,9,128]{3,2,1,0:T(8,128)}, f32[8,128]{1,0:T(8,128)}) custom-call(bf16[64,512]{1,0:T(8,128)(2,1)} %bitcast.7, bf16[2,16,512]{2,1,0:T(8,128)(2,1)} %bitcast.8, f32[1]{0:T(128)S(6)} %copy.9.e1, f32[2]{0:T(128)} %e2.1, f32[1,512]{1,0:T(1,128)} %bitcast.9, f32[8,72,512]{2,1,0:T(8,128)} %bitcast.6), custom_call_target="tpu_custom_call" | custom-call | tf_op jit(solution)/shard_map/pairs/pallas_call | solution.py:542
  109.8 4.8 %last.1 = (f32[9,36864]{1,0:T(8,128)}, f32[8,32]{1,0:T(8,128)}) custom-call(f32[2,32,9,128]{3,2,1,0:T(8,128)} %get-tuple-element.4.r_hbm, f32[64,576]{1,0:T(8,128)} %co_hbm.1, f32[8,128]{1,0:T(8,128)} %get-tuple-element.5.dens), custom_call_target="tpu_custom_call" | custom-call | tf_op jit(solution)/shard_map/last/pallas_call | solution.py:585

commit v4 on v3

--- a/solution.py
+++ b/solution.py
@@ -301,27 +301,29 @@
         for q in EARLY[right]:
             buf[0, q] = mine[q]
             q_copy(buf, 0, q, right).start()
-    for right, buf in ((True, QR), (False, QL)):
-        mine = own(lax.rem(z + (7 if right else 9), NZ))
-        for q in LATE[right]:
-            buf[1, q] = mine[q]
-            q_copy(buf, 1, q, right).start()
-        for q in EARLY[right]:
-            q_copy(buf, 0, q, right).wait_recv()
-            buf[1, q] += mine[q]
-            q_copy(buf, 1, q, right).start()
+    BUF = {True: QR, False: QL}
+    LAST = [(right, LATE[right][i]) for i in range(2) for right in (True, False)]
+    LEAD = [(right, EARLY[right][i]) for i in range(2) for right in (True, False)]
+    mine = {True: own(lax.rem(z + 7, NZ)), False: own(lax.rem(z + 9, NZ))}
+    for right, q in LAST:
+        BUF[right][1, q] = mine[right][q]
+        q_copy(BUF[right], 1, q, right).start()
+    for right, q in LEAD:
+        q_copy(BUF[right], 0, q, right).wait_recv()
+        BUF[right][1, q] += mine[right][q]
+        q_copy(BUF[right], 1, q, right).start()
 
     def q_steps(lo, hi):
         @pl.loop(lo, hi)
         def _(s):
             dr = lax.rem(z + 8 + NZ - s, NZ)
             dl = lax.rem(z + 8 + s, NZ)
-            for right, buf, d in ((True, QR, dr), (False, QL, dl)):
-                mine = own(d)
-                for q in (*EARLY[right], *LATE[right]):
-                    q_copy(buf, s - 1, q, right).wait_recv()
-                    buf[s, q] += mine[q]
-                    q_copy(buf, s, q, right).start()
+            mine = {True: own(dr), False: own(dl)}
+            for right, q in (*LAST, *LEAD):
+                buf = BUF[right]
+                q_copy(buf, s - 1, q, right).wait_recv()
+                buf[s, q] += mine[right][q]
+                q_copy(buf, s, q, right).start()
 
     for t in range(4):
         acc = dot(T[k, t * 128 : t * 128 + 128, :], AR[k], 1, 0)

time: 115 us -> 112 us (0.974)
  Pallas kernels: 113 us -> 110 us
    pallas_call x1, Pallas kernels: 109 us -> 105 us  [on_device(): pl.pallas_call(main_kernel, out_shape=(jax.ShapeDtypeStruct((2, PLANE, BR...]
where the time goes in v4:
time: 112 us; the launch traced here: 111 us
  Pallas kernels  110 us (98%)
  between operations  1.28 us (1%)
    pallas_call x1, Pallas kernels, on_device(): pl.pallas_call(main_kernel, out_shape=(jax.ShapeDtypeStruct((2, PLANE, BR...  105 us
    pallas_call x1, Pallas kernels, on_device(): pl.pallas_call(last_kernel, out_shape=(jax.ShapeDtypeStruct((BR, 36864),...  4.83 us

profile of v4, /device:TPU:1, one launch (start us, length us, event | category | flops | bytes accessed | tf_op | source)
XLA Modules:
  0.0 111.4 jit_solution(1626467344497939529)
XLA Ops:
  1.3 105.3 %pairs.1 = (f32[2,32,9,128]{3,2,1,0:T(8,128)}, f32[8,128]{1,0:T(8,128)}) custom-call(bf16[64,512]{1,0:T(8,128)(2,1)} %bitcast.7, bf16[2,16,512]{2,1,0:T(8,128)(2,1)} %bitcast.8, f32[1]{0:T(128)S(6)} %copy.9.e1, f32[2]{0:T(128)} %e2.1, f32[1,512]{1,0:T(1,128)} %bitcast.9, f32[8,72,512]{2,1,0:T(8,128)} %bitcast.6), custom_call_target="tpu_custom_call" | custom-call | tf_op jit(solution)/shard_map/pairs/pallas_call | solution.py:544
  106.5 4.8 %last.1 = (f32[9,36864]{1,0:T(8,128)}, f32[8,32]{1,0:T(8,128)}) custom-call(f32[2,32,9,128]{3,2,1,0:T(8,128)} %get-tuple-element.4.r_hbm, f32[64,576]{1,0:T(8,128)} %co_hbm.1, f32[8,128]{1,0:T(8,128)} %get-tuple-element.5.dens), custom_call_target="tpu_custom_call" | custom-call | tf_op jit(solution)/shard_map/last/pallas_call | solution.py:587
